TPU v7x, 32 devices: a whole 2x2x4 slice. The times are simulated.
32 devices in a mesh: dp: 8 (over y, x, core), mp: 4 (over z).
Axes of the slice: x: 2, y: 2, z: 4, core: 2. Of those that a mesh axis runs over, the one named last changes fastest.
Arguments:
- states: bfloat16 [512, 64, 256], P('dp', 'mp'), may hold values from -6 to 6
- key_embed: bfloat16 [512, 128], P('dp'), may hold values from -6 to 6
- partner: int32 [512], replicated, may hold values from 0 to 511, as said below
- mix_numer: int32 [512], P('dp'), may hold values from 1 to 15
- lengths: int32 [512], replicated, may hold values from 8 to 64
- w_qkv: bfloat16 [3, 256, 256], P(None, None, 'mp'), may hold values from -0.375 to 0.375
- w_out: bfloat16 [256, 256], P('mp'), may hold values from -0.375 to 0.375
- w_up: bfloat16 [256, 1024], P(None, 'mp'), may hold values from -0.375 to 0.375
- w_down: bfloat16 [1024, 256], P('mp'), may hold values from -0.1875 to 0.1875
- w_proj: bfloat16 [256, 128], replicated, may hold values from -0.375 to 0.375
Outputs:
- session_loss: float32 [512], P('dp')
- grad_states: float32 [512, 64, 256], P('dp', 'mp')
Inputs may be any that keep to these rules, and one draw needn't show every extreme that they name: partner is a permutation of the 512 sessions; a session and its partner lie in different aligned blocks of 64 sessions, and at most 10 sessions of one block have their partners in one same other block.
All inputs are finite; a program needn't handle non-finite values.
Results may differ from a plain program's by a relative error of at most 0.0091.
Values may be sent and summed in bfloat16 or wider, within the bound.
A program may use at most 64 MiB of HBM per device.

v0:
```python
import jax
import jax.numpy as jnp
from jax import lax
from jax.sharding import PartitionSpec as P

HD = 64
SOFTMAX_TEMP = 0.1
LN_EPS = 1e-05
NORM_EPS = 1e-06
TOP_PRECISION = lax.Precision.HIGHEST


def swap_rows(buffer):
    return lax.all_to_all(buffer, "dp", split_axis=0, concat_axis=0, tiled=True)


def local(states, key_embed, partner, mix_numer, lengths, w_qkv, w_out, w_up, w_down, w_proj):
    sessions_dev, ev_part, width = states.shape
    n_data = lax.axis_size("dp")
    capacity = (sessions_dev + n_data - 2) // (n_data - 1)
    device_index = lax.axis_index("dp")
    model_index = lax.axis_index("mp")
    all_keys = lax.all_gather(key_embed, "dp", axis=0, tiled=True)
    session_count = partner.shape[0]
    local_ids = jnp.arange(sessions_dev, dtype=jnp.int32)
    own_ids = device_index * sessions_dev + local_ids
    own_partner = lax.dynamic_slice_in_dim(partner, device_index * sessions_dev, sessions_dev)
    mixup_weight = mix_numer.astype(jnp.float32) / 16.0
    source = own_partner // sessions_dev
    earlier = local_ids[None, :] < local_ids[:, None]
    in_slot = jnp.sum(((source[:, None] == source[None, :]) & earlier).astype(jnp.int32), axis=1)
    wanted = partner[None, :] == own_ids[:, None]
    seeker = jnp.sum(
        jnp.where(wanted, jnp.arange(session_count, dtype=jnp.int32)[None, :], 0), axis=1
    )
    target = seeker // sessions_dev
    seeker_rows = partner.reshape(n_data, sessions_dev)[target]
    out_slot = jnp.sum(
        (
            (seeker_rows // sessions_dev == device_index)
            & (local_ids[None, :] < (seeker % sessions_dev)[:, None])
        ).astype(jnp.int32),
        axis=1,
    )
    row_len = ev_part * width
    outgoing = (
        jnp.zeros((n_data, capacity, row_len), jnp.bfloat16)
        .at[target, out_slot]
        .set(states.reshape(sessions_dev, row_len))
    )
    incoming = swap_rows(outgoing)
    partner_states = incoming[source, in_slot].reshape(sessions_dev, ev_part, width)
    mix_rows = mixup_weight[:, None, None]
    mixed_part = (
        mix_rows * states.astype(jnp.float32)
        + (1.0 - mix_rows) * partner_states.astype(jnp.float32)
    ).astype(jnp.bfloat16)
    own_lengths = lax.dynamic_slice_in_dim(lengths, device_index * sessions_dev, sessions_dev)
    len_mix = jnp.maximum(own_lengths, lengths[own_partner])
    qkv_full, out_full, up_full, down_full = (w_qkv, w_out, w_up, w_down)
    mixed = lax.all_gather(mixed_part, "mp", axis=1, tiled=True)
    layer_sessions = mixed.shape[0]
    events = mixed.shape[1]
    rows = layer_sessions * events
    positions = jnp.arange(events, dtype=jnp.int32)
    token_mask = (positions[None, :] < len_mix[:, None]).astype(jnp.float32)
    pool_weights = token_mask / len_mix[:, None].astype(jnp.float32)
    inputs_f = mixed.astype(jnp.float32).reshape(rows, width)
    row_mean = jnp.mean(inputs_f, axis=1, keepdims=True)
    centered = inputs_f - row_mean
    inv_std = lax.rsqrt(jnp.mean(centered * centered, axis=1, keepdims=True) + LN_EPS)
    unit_rows = centered * inv_std
    normed = unit_rows.astype(jnp.bfloat16)
    projected = jnp.einsum(
        "rd,jdf->jrf", normed, qkv_full, preferred_element_type=jnp.float32
    ).astype(jnp.bfloat16)
    inner_part = qkv_full.shape[2]
    heads_part = inner_part // HD
    query_h = projected[0].reshape(layer_sessions, events, heads_part, HD)
    key_h = projected[1].reshape(layer_sessions, events, heads_part, HD)
    value_h = projected[2].reshape(layer_sessions, events, heads_part, HD)
    score_scale = HD ** (-0.5)
    scores = (
        jnp.einsum("sthc,srhc->shtr", query_h, key_h, preferred_element_type=jnp.float32)
        * score_scale
    )
    exp_scores = jnp.exp(scores) * token_mask[:, None, None, :]
    probs = exp_scores / jnp.sum(exp_scores, axis=3, keepdims=True)
    probs_b = probs.astype(jnp.bfloat16)
    context = (
        jnp.einsum("shtr,srhc->sthc", probs_b, value_h, preferred_element_type=jnp.float32)
        .astype(jnp.bfloat16)
        .reshape(rows, inner_part)
    )
    pre_act = jnp.dot(normed, up_full, preferred_element_type=jnp.float32)
    hidden = jax.nn.gelu(pre_act).astype(jnp.bfloat16)
    branch = jnp.dot(context, out_full, preferred_element_type=jnp.float32) + jnp.dot(
        hidden, down_full, preferred_element_type=jnp.float32
    )
    pooled_branch = jnp.einsum(
        "st,std->sd",
        pool_weights,
        branch.reshape(layer_sessions, events, width),
        precision=TOP_PRECISION,
    )
    pooled_input = jnp.einsum(
        "st,std->sd",
        pool_weights,
        inputs_f.reshape(layer_sessions, events, width),
        precision=TOP_PRECISION,
    )
    pooled = lax.psum(pooled_branch, "mp") + pooled_input
    proj_f = w_proj.astype(jnp.float32)
    embed = jnp.dot(pooled, proj_f, precision=TOP_PRECISION)
    inv_norm = lax.rsqrt(jnp.sum(embed * embed, axis=1, keepdims=True) + NORM_EPS)
    unit_query_rows = embed * inv_norm
    keys_f = all_keys.astype(jnp.float32)
    unit_key_rows = keys_f * lax.rsqrt(jnp.sum(keys_f * keys_f, axis=1, keepdims=True) + NORM_EPS)
    pair_logits = (
        jnp.einsum("an,qn->aq", unit_query_rows, unit_key_rows, precision=TOP_PRECISION)
        / SOFTMAX_TEMP
    )
    exp_logits = jnp.exp(pair_logits)
    sum_exp = jnp.sum(exp_logits, axis=1)
    own_logit = jnp.take_along_axis(pair_logits, own_ids[:, None], axis=1)[:, 0]
    partner_logit = jnp.take_along_axis(pair_logits, own_partner[:, None], axis=1)[:, 0]
    session_loss = (
        jnp.log(sum_exp) - mixup_weight * own_logit - (1.0 - mixup_weight) * partner_logit
    )
    normalized_exponent = exp_logits / sum_exp[:, None]
    unit_gradient = (
        jnp.dot(normalized_exponent, unit_key_rows, precision=TOP_PRECISION)
        - mixup_weight[:, None] * unit_key_rows[own_ids]
        - (1.0 - mixup_weight)[:, None] * unit_key_rows[own_partner]
    ) / SOFTMAX_TEMP
    grad_embed = (
        unit_gradient
        - unit_query_rows * jnp.sum(unit_query_rows * unit_gradient, axis=1, keepdims=True)
    ) * inv_norm
    grad_pooled = jnp.einsum("se,de->sd", grad_embed, proj_f, precision=TOP_PRECISION)
    grad_full = grad_pooled[:, None, :] * pool_weights[:, :, None]
    grad_b = grad_full.reshape(rows, width).astype(jnp.bfloat16)
    d_hidden = jnp.einsum("rd,fd->rf", grad_b, down_full, preferred_element_type=jnp.float32)
    d_pre = jax.vjp(jax.nn.gelu, pre_act)[1](d_hidden)[0].astype(jnp.bfloat16)
    d_context = (
        jnp.einsum("rd,fd->rf", grad_b, out_full, preferred_element_type=jnp.float32)
        .astype(jnp.bfloat16)
        .reshape(layer_sessions, events, heads_part, HD)
    )
    d_value = jnp.einsum(
        "shtr,sthc->srhc", probs_b, d_context, preferred_element_type=jnp.float32
    ).astype(jnp.bfloat16)
    d_prob = jnp.einsum("sthc,srhc->shtr", d_context, value_h, preferred_element_type=jnp.float32)
    d_score = (
        probs * (d_prob - jnp.sum(probs * d_prob, axis=3, keepdims=True)) * score_scale
    ).astype(jnp.bfloat16)
    d_query = jnp.einsum(
        "shtr,srhc->sthc", d_score, key_h, preferred_element_type=jnp.float32
    ).astype(jnp.bfloat16)
    d_key = jnp.einsum(
        "shtr,sthc->srhc", d_score, query_h, preferred_element_type=jnp.float32
    ).astype(jnp.bfloat16)
    d_proj = jnp.stack([d_query, d_key, d_value]).reshape(3, rows, inner_part)
    d_normed = jnp.einsum(
        "jrf,jdf->rd", d_proj, qkv_full, preferred_element_type=jnp.float32
    ) + jnp.einsum("rf,df->rd", d_pre, up_full, preferred_element_type=jnp.float32)
    d_normed = d_normed.reshape(layer_sessions, events, width)
    unit_all = unit_rows.reshape(layer_sessions, events, width)
    inv_all = inv_std.reshape(layer_sessions, events, 1)
    event_start = model_index * ev_part
    unit_part = lax.dynamic_slice_in_dim(unit_all, event_start, ev_part, 1)
    inv_part = lax.dynamic_slice_in_dim(inv_all, event_start, ev_part, 1)
    d_full = lax.psum(d_normed, "mp")
    d_local = lax.dynamic_slice_in_dim(d_full, event_start, ev_part, 1)
    center = jnp.mean(d_local, axis=2, keepdims=True)
    along = jnp.mean(d_local * unit_part, axis=2, keepdims=True)
    d_mixed = (
        lax.dynamic_slice_in_dim(grad_full, event_start, ev_part, 1)
        + (d_local - center - unit_part * along) * inv_part
    )
    d_mixed_rows = d_mixed.reshape(sessions_dev, row_len)
    back_rows = ((1.0 - mixup_weight)[:, None] * d_mixed_rows).astype(jnp.bfloat16)
    returning = (
        jnp.zeros((n_data, capacity, row_len), jnp.bfloat16).at[source, in_slot].set(back_rows)
    )
    arrived = swap_rows(returning)
    grad_states = mixup_weight[:, None] * d_mixed_rows + arrived[target, out_slot].astype(
        jnp.float32
    )
    return (session_loss, grad_states.reshape(sessions_dev, ev_part, width))


def solution(mesh):
    placed = (
        P("dp", "mp", None),
        P("dp", None),
        P(),
        P("dp"),
        P(),
        P(None, None, "mp"),
        P("mp", None),
        P(None, "mp"),
        P("mp", None),
        P(),
    )
    return jax.shard_map(
        local, mesh=mesh, in_specs=placed, out_specs=(P("dp"), P("dp", "mp", None)), check_vma=False
    )
```

profile of v0, /device:TPU:0, one launch (start us, length us, event | category | flops | bytes accessed | tf_op | source)
XLA Modules:
  0.0 415.0 jit_solution(1312834488764694528)
XLA Ops:
  12.3 9.7 %scatter_fusion = bf16[8,10,4096]{2,0,1:T(8,128)(2,1)S(1)} fusion(bf16[8,10,4096]{2,0,1:T(8,128)(2,1)S(1)} %broadcast.348.clone, s32[64]{0:T(128)S(1)} %get-tuple-element.15, bf16[64,4096]{1,0:T(8,128)(2,1)S(1)} %bitcast.216), kind=kCustom, calls=%fused_computation.8 | custom fusion | bytes 1573376 | tf_op jit(solution)/shard_map/scatter | solution.py:49
  23.4 5.2 %all-to-all-start = ((bf16[8,10,4096]{2,1,0:T(8,128)(2,1)}), bf16[8,10,4096]{2,1,0:T(8,128)(2,1)S(1)}, u32[]{:S(2)}, u32[]{:S(2)}) async-start(bf16[8,10,4096]{2,1,0:T(8,128)(2,1)} %copy.60), calls=%async_computation | async-start | bytes 2097152 | tf_op jit(solution)/shard_map/all_to_all | solution.py:14
  28.8 15.1 %all-to-all-done = bf16[8,10,4096]{2,1,0:T(8,128)(2,1)S(1)} async-done(((bf16[8,10,4096]{2,1,0:T(8,128)(2,1)}), bf16[8,10,4096]{2,1,0:T(8,128)(2,1)S(1)}, u32[]{:S(2)}, u32[]{:S(2)}) %all-to-all-start) | async-done | bytes 655392 | tf_op jit(solution)/shard_map/all_to_all | solution.py:14
  44.3 2.2 gather_fusion.2
  49.5 8.2 %all_gather.7 = bf16[512,128]{1,0:T(8,128)(2,1)S(1)} all-gather(bf16[64,128]{1,0:T(8,128)(2,1)S(1)} %copy-done.17), channel_id=1, replica_groups=mesh['dp'=8,'mp'=4] {'dp'}, dimensions={0}, use_global_device_ids=true | all-gather | bytes 147456 | tf_op jit(solution)/shard_map/all_gather | solution.py:23
  61.1 31.9 %all-gather.2.cloned.1.call-done = bf16[64,64,256]{2,1,0:T(8,128)(2,1)} async-done(((bf16[64,16,256]{2,1,0:T(8,128)(2,1)}), bf16[64,64,256]{2,1,0:T(8,128)(2,1)}) %all-gather.2.cloned.1.call-update) | async-done | bytes 2097168 | tf_op jit(solution)/shard_map/all_gather | solution.py:61
  93.0 2.4 convert_reduce_fusion
  95.4 3.1 broadcast_subtract_fusion
  98.6 2.5 fusion.10
  103.1 2.1 reshape.404
  105.1 2.1 reshape.403
  108.9 3.7 fusion.132
  112.6 5.0 %fusion.26 = (f32[64,64]{1,0:T(8,128)S(1)}, f32[64,64,64]{1,2,0:T(8,128)S(1)}) fusion(f32[64,64]{1,0:T(8,128)S(1)} %copy-done.15, bf16[64,64,64]{1,0,2:T(8,128)(2,1)S(1)} %copy-done.9, bf16[64,64,64]{1,0,2:T(8,128)(2,1)S(1)} %copy-done.7), kind=kOutput, calls=%fused_computation.48 | convolution fusion | flops 34336768 | bytes 2129920 | tf_op jit(solution)/shard_map/sthc,srhc->shtr/dot_general | solution.py:84
  122.7 1.9 convolution_add_fusion.1
  124.7 2.1 fusion.133
  129.2 31.5 %all-reduce.3.cloned.1.call-done = f32[64,256]{1,0:T(8,128)} async-done(((f32[64,256]{1,0:T(8,128)}), f32[64,256]{1,0:T(8,128)}) %all-reduce.3.cloned.1.call-update) | async-done | bytes 65552 | tf_op jit(solution)/shard_map/psum | solution.py:112
  167.9 2.8 reshape.407
  170.7 3.8 fusion.58
  174.5 3.4 fusion.45
  177.8 6.9 %fusion.49 = bf16[64,64,1,64]{1,3,0,2:T(8,128)(2,1)} fusion(f32[64,64,64]{1,2,0:T(8,128)} %fusion.58, bf16[64,64,64]{1,0,2:T(8,128)(2,1)} %reshape.404, f32[64,64,64]{1,2,0:T(8,128)} %copy-done.27, f32[64,64]{1,0:T(8,128)} %copy-done.29, f32[64,64]{1,0:T(8,128)} %fusion.80), kind=kOutput, calls=%fused_computation.64 | convolution fusion | flops 36704320 | bytes 3178496 | tf_op jit(solution)/shard_map/shtr,srhc->sthc/dot_general | solution.py:157
  184.7 7.8 %fusion.46 = bf16[64,64,1,64]{1,3,0,2:T(8,128)(2,1)} fusion(f32[64,64,64]{1,2,0:T(8,128)} %fusion.58, bf16[64,64,64]{1,0,2:T(8,128)(2,1)S(1)} %copy-done.8, f32[64,64,64]{1,2,0:T(8,128)} %copy-done.27, f32[64,64]{1,0:T(8,128)} %copy-done.29, f32[64,64]{1,0:T(8,128)} %fusion.80), kind=kOutput, calls=%fused_computation.63 | convolution fusion | flops 36704320 | bytes 3178496 | tf_op jit(solution)/shard_map/shtr,sthc->srhc/dot_general | solution.py:160
  192.5 1.9 copy.77
  196.1 1.9 copy.74
  203.1 4.1 convolution_bitcast_fusion
  207.3 7.0 %convolution_add_fusion = f32[4096,256]{1,0:T(8,128)} fusion(f32[4096,256]{1,0:T(8,128)} %convolution_bitcast_fusion, bf16[256,256]{1,0:T(8,128)(2,1)S(1)} %copy-done.11, f32[4096,256]{1,0:T(8,128)} %fusion.132, bf16[4096,256]{1,0:T(8,128)(2,1)S(1)} %fusion.8, bf16[256,256]{1,0:T(8,128)(2,1)S(1)} %copy-done), kind=kOutput, calls=%fused_computation.13 | convolution fusion | flops 1095761920 | bytes 14942208 | tf_op jit(solution)/shard_map/rf,df->rd/dot_general | solution.py:166
  214.4 154.6 %all-reduce.5.cloned.1.call-done = f32[64,64,256]{2,1,0:T(8,128)} async-done(((f32[64,64,256]{2,1,0:T(8,128)}), f32[64,64,256]{2,1,0:T(8,128)}) %all-reduce.5.cloned.1.call-update) | async-done | bytes 4194320 | tf_op jit(solution)/shard_map/psum | solution.py:173
  369.1 2.1 dynamic-slice_reduce_fusion
  371.2 2.0 multiply_add_fusion
  374.0 9.7 %scatter_fusion.1 = bf16[8,10,4096]{2,0,1:T(8,128)(2,1)S(1)} fusion(bf16[8,10,4096]{2,0,1:T(8,128)(2,1)S(1)} %broadcast.348, s32[64]{0:T(128)S(1)} %get-tuple-element.16, bf16[64,4096]{1,0:T(8,128)(2,1)S(1)} %multiply_convert_fusion.3), kind=kCustom, calls=%fused_computation.9 | custom fusion | bytes 1573376 | tf_op jit(solution)/shard_map/scatter | solution.py:184
  385.1 3.9 all-to-all-start.1
  391.4 13.0 %all-to-all-done.1 = bf16[8,10,4096]{2,1,0:T(8,128)(2,1)S(1)} async-done(((bf16[8,10,4096]{2,1,0:T(8,128)(2,1)}), bf16[8,10,4096]{2,1,0:T(8,128)(2,1)S(1)}, u32[]{:S(2)}, u32[]{:S(2)}) %all-to-all-start.1) | async-done | bytes 655392 | tf_op jit(solution)/shard_map/all_to_all | solution.py:14
  404.7 2.2 gather_fusion.5
  (143 shorter events, 44.6 us)
Async XLA Ops:
  7.2 114.1 %copy-start = (bf16[256,256]{1,0:T(8,128)(2,1)S(1)}, bf16[256,256]{1,0:T(8,128)(2,1)}, u32[]{:S(2)}) copy-start(bf16[256,256]{1,0:T(8,128)(2,1)} %param.20) | copy-start | bytes 393220
  22.0 6.8 %copy-start.25 = (s32[64]{0:T(128)S(1)}, s32[64]{0:T(128)}, u32[]{:S(2)}) copy-start(s32[64]{0:T(128)} %param.15) | copy-start | bytes 772
  23.4 20.6 %all-to-all-start = ((bf16[8,10,4096]{2,1,0:T(8,128)(2,1)}), bf16[8,10,4096]{2,1,0:T(8,128)(2,1)S(1)}, u32[]{:S(2)}, u32[]{:S(2)}) async-start(bf16[8,10,4096]{2,1,0:T(8,128)(2,1)} %copy.60), calls=%async_computation | async-start | bytes 2097152 | tf_op jit(solution)/shard_map/all_to_all | solution.py:14
  28.6 64.4 %all-gather.2.cloned.1.call-start = ((), (), s32[]{:S(2)}) async-start(), calls=%async_computation.2 | async-start | bytes 2621440 | tf_op jit(solution)/shard_map/all_gather | solution.py:61
  28.8 17.9 %copy-start.21 = (f32[64]{0:T(128)}, f32[64]{0:T(128)S(1)}, u32[]{:S(2)}) copy-start(f32[64]{0:T(128)S(1)} %get-tuple-element.21) | copy-start | bytes 772
  28.8 17.9 %copy-start.23 = (f32[64]{0:T(128)}, f32[64]{0:T(128)S(1)}, u32[]{:S(2)}) copy-start(f32[64]{0:T(128)S(1)} %get-tuple-element.20) | copy-start | bytes 772
  44.3 2.4 copy-start.6
  46.5 3.0 copy-start.17
  47.8 112.9 %all-reduce.3.cloned.1.call-start = ((), (), s32[]{:S(2)}) async-start(), calls=%async_computation.3 | async-start | bytes 131072 | tf_op jit(solution)/shard_map/psum | solution.py:112
  93.0 2.4 copy-start.2
  98.6 2.5 copy-start.14
  108.8 3.8 copy-start.7
  108.8 3.8 copy-start.9
  108.8 3.8 copy-start.15
  119.0 1.5 copy-start.12
  120.5 2.2 copy-start.4
  124.7 3.0 copy-start.3
  127.4 33.3 %copy-start.10 = (bf16[256,128]{1,0:T(8,128)(2,1)S(1)}, bf16[256,128]{1,0:T(8,128)(2,1)}, u32[]{:S(2)}) copy-start(bf16[256,128]{1,0:T(8,128)(2,1)} %param.21) | copy-start | bytes 196612
  127.4 241.6 %all-reduce.5.cloned.1.call-start = ((), (), s32[]{:S(2)}) async-start(), calls=%async_computation.4 | async-start | bytes 8388608 | tf_op jit(solution)/shard_map/psum | solution.py:173
  160.7 5.6 %copy-start.13 = (bf16[64,256]{1,0:T(8,128)(2,1)S(1)}, bf16[64,256]{1,0:T(8,128)(2,1)}, u32[]{:S(2)}) copy-start(bf16[64,256]{1,0:T(8,128)(2,1)} %param.18) | copy-start | bytes 98308
  170.7 3.8 copy-start.5
  170.7 3.8 copy-start.16
  170.7 3.8 copy-start.28
  170.7 3.8 copy-start.30
  177.8 6.9 %copy-start.8 = (bf16[64,64,64]{1,0,2:T(8,128)(2,1)S(1)}, bf16[64,64,64]{1,0,2:T(8,128)(2,1)}, u32[]{:S(2)}) copy-start(bf16[64,64,64]{1,0,2:T(8,128)(2,1)} %reshape.403) | copy-start | bytes 1572868
  203.1 4.1 copy-start.11
  371.2 2.6 copy-start.22
  383.7 5.4 %copy-start.20 = (s32[64,1,1]{0,2,1:T(1,128)S(1)}, s32[64,1,1]{0,2,1:T(1,128)}, u32[]{:S(2)}) copy-start(s32[64,1,1]{0,2,1:T(1,128)} %get-tuple-element.5) | copy-start | bytes 772
  383.7 7.2 %copy-start.19 = (f32[64]{0:T(128)S(1)}, f32[64]{0:T(128)}, u32[]{:S(2)}) copy-start(f32[64]{0:T(128)} %copy-done.18) | copy-start | bytes 772
  383.7 7.2 %copy-start.26 = (s32[64]{0:T(128)S(1)}, s32[64]{0:T(128)}, u32[]{:S(2)}) copy-start(s32[64]{0:T(128)} %param.15) | copy-start | bytes 772
  385.1 19.3 %all-to-all-start.1 = ((bf16[8,10,4096]{2,1,0:T(8,128)(2,1)}), bf16[8,10,4096]{2,1,0:T(8,128)(2,1)S(1)}, u32[]{:S(2)}, u32[]{:S(2)}) async-start(bf16[8,10,4096]{2,1,0:T(8,128)(2,1)} %copy.78), calls=%async_computation.1 | async-start | bytes 2097152 | tf_op jit(solution)/shard_map/all_to_all | solution.py:14
  404.7 2.4 copy-start.24
  (4 other events, 5.3 us)
Sparse Core Ops, SparseCore 0:
  47.9 45.0 all-gather.1
  127.6 33.0 all-reduce.2
  214.4 154.6 all-reduce.4
where the time goes:
time: 422 us; the launch traced here: 415 us
  waiting for transfers between devices  246 us (58%)
  local copies, waits for them, and re-layouts  60.4 us (14%)
  matrix products  55.9 us (13%)
  other arithmetic  20.1 us (5%)
  between operations  14.7 us (3%)
  starting transfers between devices  9.43 us (2%)
  blocking collectives  8.24 us (2%)
    psum x1, waiting for transfers between devices, local(): d_full = lax.psum(d_normed, 'mp')  155 us
    all_gather x1, waiting for transfers between devices, local(): mixed = lax.all_gather(mixed_part, 'mp', axis=1, tiled=True)  31.9 us
    psum x1, waiting for transfers between devices, local(): pooled = lax.psum(pooled_branch, 'mp') + pooled_input  31.5 us
    all_to_all x2, waiting for transfers between devices, swap_rows(): return lax.all_to_all(buffer, 'dp', split_axis=0, concat_axis=0, tiled=True)  28.1 us
    scatter x2, local copies, waits for them, and re-layouts, local(): outgoing = jnp.zeros((n_data, capacity, row_len), jnp.bfloat16).at[target...  11.1 us
    scatter x2, local copies, waits for them, and re-layouts, local(): jnp.zeros((n_data, capacity, row_len), jnp.bfloat16).at[source, in_slot]  11.1 us
    all_to_all x2, starting transfers between devices, swap_rows(): return lax.all_to_all(buffer, 'dp', split_axis=0, concat_axis=0, tiled=True)  9.13 us
    another operation x6, local copies, waits for them, and re-layouts  8.6 us
  transfers between devices with their start and end apart: 5, of which 5 were waited for; matrix products, arithmetic and copies ran while one was open for 2% of the time, Pallas kernels for 0%

commit v1 on v0

--- a/solution.py
+++ b/solution.py
@@ -58,7 +58,12 @@
     own_lengths = lax.dynamic_slice_in_dim(lengths, device_index * sessions_dev, sessions_dev)
     len_mix = jnp.maximum(own_lengths, lengths[own_partner])
     qkv_full, out_full, up_full, down_full = (w_qkv, w_out, w_up, w_down)
-    mixed = lax.all_gather(mixed_part, "mp", axis=1, tiled=True)
+    ring = [mixed_part]
+    for hop in range(3):
+        ring.append(lax.ppermute(ring[-1], "mp", [(dev, (dev + 1) % 4) for dev in range(4)]))
+    mixed = jnp.roll(
+        jnp.concatenate(ring[::-1], axis=1), (lax.axis_index("mp") + 1) * ring[0].shape[1], axis=1
+    )
     layer_sessions = mixed.shape[0]
     events = mixed.shape[1]
     rows = layer_sessions * events

time: 422 us -> 419 us (level)
  waiting for transfers between devices: 246 us -> 241 us
    all_gather x1 -> x0, waiting for transfers between devices: 31.9 us -> none  [local(): mixed = lax.all_gather(mixed_part, 'mp', axis=1, tiled=True)]
    ppermute x0 -> x3, waiting for transfers between devices: none -> 24.9 us  [local(): lax.ppermute(ring[-1], 'mp', [(dev, (dev + 1) % 4) for dev in range(4)])]
  transfers between devices with their start and end apart: 5 -> 7, of which waited for: 5 -> 7; matrix products, arithmetic and copies ran while one was open for 2% -> 2% of each run, Pallas kernels for 0% -> 0%
where the time goes in v1:
time: 419 us; the launch traced here: 412 us
  waiting for transfers between devices  241 us (58%)
  local copies, waits for them, and re-layouts  63 us (15%)
  matrix products  54.9 us (13%)
  other arithmetic  18.9 us (5%)
  between operations  15.1 us (4%)
  starting transfers between devices  11 us (3%)
  blocking collectives  8.25 us (2%)
    psum x1, waiting for transfers between devices, local(): d_full = lax.psum(d_normed, 'mp')  155 us
    psum x1, waiting for transfers between devices, local(): pooled = lax.psum(pooled_branch, 'mp') + pooled_input  32.9 us
    all_to_all x2, waiting for transfers between devices, swap_rows(): return lax.all_to_all(buffer, 'dp', split_axis=0, concat_axis=0, tiled=True)  28.1 us
    ppermute x3, waiting for transfers between devices, local(): lax.ppermute(ring[-1], 'mp', [(dev, (dev + 1) % 4) for dev in range(4)])  24.9 us
    scatter x2, local copies, waits for them, and re-layouts, local(): outgoing = jnp.zeros((n_data, capacity, row_len), jnp.bfloat16).at[target...  11.1 us
    scatter x2, local copies, waits for them, and re-layouts, local(): jnp.zeros((n_data, capacity, row_len), jnp.bfloat16).at[source, in_slot]  11.1 us
    all_to_all x2, starting transfers between devices, swap_rows(): return lax.all_to_all(buffer, 'dp', split_axis=0, concat_axis=0, tiled=True)  9.13 us
    another operation x6, local copies, waits for them, and re-layouts  8.54 us
  transfers between devices with their start and end apart: 7, of which 7 were waited for; matrix products, arithmetic and copies ran while one was open for 2% of the time, Pallas kernels for 0%

profile of v1, /device:TPU:0, one launch (start us, length us, event | category | flops | bytes accessed | tf_op | source)
XLA Modules:
  0.0 411.7 jit_solution(18122296024606854064)
XLA Ops:
  12.3 9.7 %scatter_fusion = bf16[8,10,4096]{2,0,1:T(8,128)(2,1)S(1)} fusion(bf16[8,10,4096]{2,0,1:T(8,128)(2,1)S(1)} %broadcast.355.clone, s32[64]{0:T(128)S(1)} %get-tuple-element.15, bf16[64,4096]{1,0:T(8,128)(2,1)S(1)} %bitcast.215), kind=kCustom, calls=%fused_computation.8 | custom fusion | bytes 1573376 | tf_op jit(solution)/shard_map/scatter | solution.py:49
  23.4 5.2 %all-to-all-start = ((bf16[8,10,4096]{2,1,0:T(8,128)(2,1)}), bf16[8,10,4096]{2,1,0:T(8,128)(2,1)S(1)}, u32[]{:S(2)}, u32[]{:S(2)}) async-start(bf16[8,10,4096]{2,1,0:T(8,128)(2,1)} %copy.60), calls=%async_computation | async-start | bytes 2097152 | tf_op jit(solution)/shard_map/all_to_all | solution.py:14
  28.8 15.1 %all-to-all-done = bf16[8,10,4096]{2,1,0:T(8,128)(2,1)S(1)} async-done(((bf16[8,10,4096]{2,1,0:T(8,128)(2,1)}), bf16[8,10,4096]{2,1,0:T(8,128)(2,1)S(1)}, u32[]{:S(2)}, u32[]{:S(2)}) %all-to-all-start) | async-done | bytes 655392 | tf_op jit(solution)/shard_map/all_to_all | solution.py:14
  44.3 2.2 gather_fusion.2
  49.4 8.2 %all_gather.3 = bf16[512,128]{1,0:T(8,128)(2,1)S(1)} all-gather(bf16[64,128]{1,0:T(8,128)(2,1)S(1)} %copy-done.18), channel_id=1, replica_groups=mesh['dp'=8,'mp'=4] {'dp'}, dimensions={0}, use_global_device_ids=true | all-gather | bytes 147456 | tf_op jit(solution)/shard_map/all_gather | solution.py:23
  57.7 2.1 collective-permute-done
  60.1 13.6 %collective-permute-done.1 = bf16[64,16,256]{2,1,0:T(8,128)(2,1)S(1)} collective-permute-done((bf16[64,16,256]{2,1,0:T(8,128)(2,1)S(1)}, bf16[64,16,256]{2,1,0:T(8,128)(2,1)S(1)}, u32[]{:S(2)}, u32[]{:S(2)}) %collective-permute-start.1) | collective-permute-done | bytes 524320 | tf_op jit(solution)/shard_map/ppermute | solution.py:63
  77.6 9.2 %collective-permute-done.2 = bf16[64,16,256]{2,1,0:T(8,128)(2,1)S(1)} collective-permute-done((bf16[64,16,256]{2,1,0:T(8,128)(2,1)S(1)}, bf16[64,16,256]{2,1,0:T(8,128)(2,1)S(1)}, u32[]{:S(2)}, u32[]{:S(2)}) %collective-permute-start.2) | collective-permute-done | bytes 524320 | tf_op jit(solution)/shard_map/ppermute | solution.py:63
  87.4 2.0 copy-done.3
  90.1 4.3 %broadcast_subtract_fusion = (f32[64,64,256]{2,1,0:T(8,128)}, f32[64,64]{1,0:T(8,128)S(1)}) fusion(f32[64,64]{1,0:T(8,128)S(1)} %broadcast_multiply_fusion.2, bf16[64,128,256]{2,1,0:T(8,128)(2,1)} %copy-done.3, s32[]{:T(128)S(6)} %select_n.129), kind=kLoop, calls=%fused_computation.45 | loop fusion | flops 4190208 | bytes 6324228 | tf_op jit(solution)/shard_map/sub | solution.py:75
  94.4 2.5 fusion.10
  98.9 2.1 reshape.404
  101.0 2.1 reshape.403
  104.7 3.7 fusion.135
  108.4 5.0 %fusion.26 = (f32[64,64]{1,0:T(8,128)S(1)}, f32[64,64,64]{1,2,0:T(8,128)S(1)}) fusion(f32[64,64]{1,0:T(8,128)S(1)} %copy-done.16, bf16[64,64,64]{1,0,2:T(8,128)(2,1)S(1)} %copy-done.8, bf16[64,64,64]{1,0,2:T(8,128)(2,1)S(1)} %copy-done.6), kind=kOutput, calls=%fused_computation.48 | convolution fusion | flops 34336768 | bytes 2129920 | tf_op jit(solution)/shard_map/sthc,srhc->shtr/dot_general | solution.py:89
  120.5 2.1 fusion.136
  123.5 2.5 fusion.52
  126.0 32.9 %all-reduce.3.cloned.1.call-done = f32[64,256]{1,0:T(8,128)} async-done(((f32[64,256]{1,0:T(8,128)}), f32[64,256]{1,0:T(8,128)}) %all-reduce.3.cloned.1.call-update) | async-done | bytes 65552 | tf_op jit(solution)/shard_map/psum | solution.py:117
  164.5 2.8 reshape.407
  167.3 3.8 fusion.60
  171.1 3.4 fusion.45
  174.5 6.9 %fusion.49 = bf16[64,64,1,64]{1,3,0,2:T(8,128)(2,1)} fusion(f32[64,64,64]{1,2,0:T(8,128)} %fusion.60, bf16[64,64,64]{1,0,2:T(8,128)(2,1)} %reshape.404, f32[64,64,64]{1,2,0:T(8,128)} %copy-done.30, f32[64,64]{1,0:T(8,128)} %copy-done.32, f32[64,64]{1,0:T(8,128)} %fusion.82), kind=kOutput, calls=%fused_computation.64 | convolution fusion | flops 36704320 | bytes 3178496 | tf_op jit(solution)/shard_map/shtr,srhc->sthc/dot_general | solution.py:162
  181.3 7.5 %fusion.46 = bf16[64,64,1,64]{1,3,0,2:T(8,128)(2,1)} fusion(f32[64,64,64]{1,2,0:T(8,128)} %fusion.60, bf16[64,64,64]{1,0,2:T(8,128)(2,1)S(1)} %copy-done.7, f32[64,64,64]{1,2,0:T(8,128)} %copy-done.30, f32[64,64]{1,0:T(8,128)} %copy-done.32, f32[64,64]{1,0:T(8,128)} %fusion.82), kind=kOutput, calls=%fused_computation.63 | convolution fusion | flops 36704320 | bytes 3178496 | tf_op jit(solution)/shard_map/shtr,sthc->srhc/dot_general | solution.py:165
  199.4 4.1 %convolution_bitcast_fusion = f32[4096,256]{1,0:T(8,128)} fusion(bf16[3,256,64]{1,2,0:T(8,128)(2,1)} %param.17, bf16[1,4096,64]{1,2,0:T(8,128)(2,1)} %stack.14, bf16[1,4096,64]{1,2,0:T(8,128)(2,1)} %stack.13, bf16[1,4096,64]{1,2,0:T(8,128)(2,1)} %stack.12), kind=kOutput, calls=%fused_computation.14 | convolution fusion | flops 404226048 | bytes 5865472 | tf_op jit(solution)/shard_map/jrf,jdf->rd/dot_general | solution.py:169
  203.6 7.0 %convolution_add_fusion = f32[4096,256]{1,0:T(8,128)} fusion(f32[4096,256]{1,0:T(8,128)} %convolution_bitcast_fusion, bf16[256,256]{1,0:T(8,128)(2,1)S(1)} %copy-done.10, f32[4096,256]{1,0:T(8,128)} %fusion.135, bf16[4096,256]{1,0:T(8,128)(2,1)S(1)} %fusion.8, bf16[256,256]{1,0:T(8,128)(2,1)S(1)} %copy-done), kind=kOutput, calls=%fused_computation.13 | convolution fusion | flops 1095761920 | bytes 14942208 | tf_op jit(solution)/shard_map/rf,df->rd/dot_general | solution.py:171
  210.7 154.7 %all-reduce.5.cloned.1.call-done = f32[64,64,256]{2,1,0:T(8,128)} async-done(((f32[64,64,256]{2,1,0:T(8,128)}), f32[64,64,256]{2,1,0:T(8,128)}) %all-reduce.5.cloned.1.call-update) | async-done | bytes 4194320 | tf_op jit(solution)/shard_map/psum | solution.py:178
  365.4 2.1 dynamic-slice_reduce_fusion
  367.5 2.0 multiply_add_fusion
  370.3 9.7 %scatter_fusion.1 = bf16[8,10,4096]{2,0,1:T(8,128)(2,1)S(1)} fusion(bf16[8,10,4096]{2,0,1:T(8,128)(2,1)S(1)} %broadcast.355, s32[64]{0:T(128)S(1)} %get-tuple-element.16, bf16[64,4096]{1,0:T(8,128)(2,1)S(1)} %multiply_convert_fusion.3), kind=kCustom, calls=%fused_computation.9 | custom fusion | bytes 1573376 | tf_op jit(solution)/shard_map/scatter | solution.py:189
  381.4 3.9 all-to-all-start.1
  387.7 13.0 %all-to-all-done.1 = bf16[8,10,4096]{2,1,0:T(8,128)(2,1)S(1)} async-done(((bf16[8,10,4096]{2,1,0:T(8,128)(2,1)}), bf16[8,10,4096]{2,1,0:T(8,128)(2,1)S(1)}, u32[]{:S(2)}, u32[]{:S(2)}) %all-to-all-start.1) | async-done | bytes 655392 | tf_op jit(solution)/shard_map/all_to_all | solution.py:14
  401.1 2.2 gather_fusion.5
  (160 shorter events, 49.1 us)
Async XLA Ops:
  7.2 109.9 %copy-start = (bf16[256,256]{1,0:T(8,128)(2,1)S(1)}, bf16[256,256]{1,0:T(8,128)(2,1)}, u32[]{:S(2)}) copy-start(bf16[256,256]{1,0:T(8,128)(2,1)} %param.20) | copy-start | bytes 393220
  22.0 6.8 %copy-start.28 = (s32[64]{0:T(128)S(1)}, s32[64]{0:T(128)}, u32[]{:S(2)}) copy-start(s32[64]{0:T(128)} %param.15) | copy-start | bytes 772
  23.4 20.6 %all-to-all-start = ((bf16[8,10,4096]{2,1,0:T(8,128)(2,1)}), bf16[8,10,4096]{2,1,0:T(8,128)(2,1)S(1)}, u32[]{:S(2)}, u32[]{:S(2)}) async-start(bf16[8,10,4096]{2,1,0:T(8,128)(2,1)} %copy.60), calls=%async_computation | async-start | bytes 2097152 | tf_op jit(solution)/shard_map/all_to_all | solution.py:14
  28.6 130.4 %all-reduce.3.cloned.1.call-start = ((), (), s32[]{:S(2)}) async-start(), calls=%async_computation.2 | async-start | bytes 131072 | tf_op jit(solution)/shard_map/psum | solution.py:117
  28.8 17.9 %copy-start.22 = (f32[64]{0:T(128)}, f32[64]{0:T(128)S(1)}, u32[]{:S(2)}) copy-start(f32[64]{0:T(128)S(1)} %get-tuple-element.21) | copy-start | bytes 772
  28.8 17.9 %copy-start.25 = (f32[64]{0:T(128)}, f32[64]{0:T(128)S(1)}, u32[]{:S(2)}) copy-start(f32[64]{0:T(128)S(1)} %get-tuple-element.20) | copy-start | bytes 772
  46.5 2.9 copy-start.18
  47.0 12.8 %collective-permute-start = (bf16[64,16,256]{2,1,0:T(8,128)(2,1)S(1)}, bf16[64,16,256]{2,1,0:T(8,128)(2,1)S(1)}, u32[]{:S(2)}, u32[]{:S(2)}) collective-permute-start(bf16[64,16,256]{2,1,0:T(8,128)(2,1)S(1)} %fusion.57), channel_id=1, source_target_pairs={{0,1},{1,2},{2,3},{3,0},{4,5},{5,6},{6,7},{7,4},{8,9},{9,10},{10,1... | collective-permute-start | bytes 1572872 | tf_op jit(solution)/shard_map/ppermute | solution.py:63
  59.8 13.9 %collective-permute-start.1 = (bf16[64,16,256]{2,1,0:T(8,128)(2,1)S(1)}, bf16[64,16,256]{2,1,0:T(8,128)(2,1)S(1)}, u32[]{:S(2)}, u32[]{:S(2)}) collective-permute-start(bf16[64,16,256]{2,1,0:T(8,128)(2,1)S(1)} %collective-permute-done), channel_id=1, source_target_pairs={{0,1},{1,2},{2,3},{3,0},{4,5},{5,6},{6,7},{7,4},{8,9},{9,10},{10,1... | collective-permute-start | bytes 1572872 | tf_op jit(solution)/shard_map/ppermute | solution.py:63
  73.7 13.1 %collective-permute-start.2 = (bf16[64,16,256]{2,1,0:T(8,128)(2,1)S(1)}, bf16[64,16,256]{2,1,0:T(8,128)(2,1)S(1)}, u32[]{:S(2)}, u32[]{:S(2)}) collective-permute-start(bf16[64,16,256]{2,1,0:T(8,128)(2,1)S(1)} %collective-permute-done.1), channel_id=1, source_target_pairs={{0,1},{1,2},{2,3},{3,0},{4,5},{5,6},{6,7},{7,4},{8,9},{9,10},{10,1... | collective-permute-start | bytes 1572872 | tf_op jit(solution)/shard_map/ppermute | solution.py:63
  94.4 2.5 copy-start.13
  104.6 3.8 copy-start.6
  104.6 3.7 copy-start.8
  104.7 3.7 copy-start.16
  122.6 36.4 %copy-start.9 = (bf16[256,128]{1,0:T(8,128)(2,1)S(1)}, bf16[256,128]{1,0:T(8,128)(2,1)}, u32[]{:S(2)}) copy-start(bf16[256,128]{1,0:T(8,128)(2,1)} %param.21) | copy-start | bytes 196612
  122.6 38.1 %copy-start.14 = (f32[64,128]{1,0:T(8,128)S(1)}, f32[64,128]{1,0:T(8,128)}, u32[]{:S(2)}) copy-start(f32[64,128]{1,0:T(8,128)} %gather_fusion.4) | copy-start | bytes 98308
  122.6 38.1 %copy-start.15 = (f32[64,128]{1,0:T(8,128)S(1)}, f32[64,128]{1,0:T(8,128)}, u32[]{:S(2)}) copy-start(f32[64,128]{1,0:T(8,128)} %gather_fusion.3) | copy-start | bytes 98308
  122.6 38.1 %copy-start.23 = (f32[64]{0:T(128)S(1)}, f32[64]{0:T(128)}, u32[]{:S(2)}) copy-start(f32[64]{0:T(128)} %copy-done.22) | copy-start | bytes 772
  122.6 38.1 %copy-start.26 = (f32[64]{0:T(128)S(1)}, f32[64]{0:T(128)}, u32[]{:S(2)}) copy-start(f32[64]{0:T(128)} %copy-done.25) | copy-start | bytes 772
  123.3 242.1 %all-reduce.5.cloned.1.call-start = ((), (), s32[]{:S(2)}) async-start(), calls=%async_computation.3 | async-start | bytes 8388608 | tf_op jit(solution)/shard_map/psum | solution.py:178
  159.0 4.0 copy-start.12
  167.3 3.8 copy-start.4
  167.3 3.8 copy-start.17
  167.3 3.8 copy-start.31
  167.3 3.8 copy-start.33
  174.5 6.9 %copy-start.7 = (bf16[64,64,64]{1,0,2:T(8,128)(2,1)S(1)}, bf16[64,64,64]{1,0,2:T(8,128)(2,1)}, u32[]{:S(2)}) copy-start(bf16[64,64,64]{1,0,2:T(8,128)(2,1)} %reshape.403) | copy-start | bytes 1572868
  199.4 4.1 %copy-start.10 = (bf16[256,256]{1,0:T(8,128)(2,1)S(1)}, bf16[256,256]{1,0:T(8,128)(2,1)}, u32[]{:S(2)}) copy-start(bf16[256,256]{1,0:T(8,128)(2,1)} %param.19) | copy-start | bytes 393220
  367.5 2.6 copy-start.24
  380.0 5.4 %copy-start.21 = (s32[64,1,1]{0,2,1:T(1,128)S(1)}, s32[64,1,1]{0,2,1:T(1,128)}, u32[]{:S(2)}) copy-start(s32[64,1,1]{0,2,1:T(1,128)} %get-tuple-element.5) | copy-start | bytes 772
  380.0 7.2 %copy-start.20 = (f32[64]{0:T(128)S(1)}, f32[64]{0:T(128)}, u32[]{:S(2)}) copy-start(f32[64]{0:T(128)} %copy-done.19) | copy-start | bytes 772
  380.0 7.2 %copy-start.29 = (s32[64]{0:T(128)S(1)}, s32[64]{0:T(128)}, u32[]{:S(2)}) copy-start(s32[64]{0:T(128)} %param.15) | copy-start | bytes 772
  381.4 19.3 %all-to-all-start.1 = ((bf16[8,10,4096]{2,1,0:T(8,128)(2,1)}), bf16[8,10,4096]{2,1,0:T(8,128)(2,1)S(1)}, u32[]{:S(2)}, u32[]{:S(2)}) async-start(bf16[8,10,4096]{2,1,0:T(8,128)(2,1)} %copy.78), calls=%async_computation.1 | async-start | bytes 2097152 | tf_op jit(solution)/shard_map/all_to_all | solution.py:14
  (9 other events, 15.8 us)
Sparse Core Ops, SparseCore 0:
  123.4 35.5 all-reduce.2
  210.7 154.6 all-reduce.4
